TPU v7x, 512 devices: a whole 4x4x16 slice. The times are simulated.
512 devices in a mesh: ctx: 64 (over z, y), tp: 8 (over x, core).
Axes of the slice: x: 4, y: 4, z: 16, core: 2. Of those that a mesh axis runs over, the one named last changes fastest.
Arguments:
- queries: bfloat16 [8192, 4096], P('ctx', 'tp'), may hold values from -6 to 6
- keys: bfloat16 [8192, 1024], P('ctx', 'tp'), may hold values from -6 to 6
- values: bfloat16 [8192, 1024], P('ctx', 'tp'), may hold values from -4 to 4
- w_out: bfloat16 [4096, 4096], P('tp'), may hold values from -0.09375 to 0.09375
- relevance_out: bfloat16 [8192, 4096], P('ctx', 'tp'), may hold values from -4 to 4
- segment_ids: int32 [8192], replicated, may hold values from 0 to 31, never falling along the last dimension, each value on 1 to 1024 neighbouring positions
Outputs:
- relevance_heads: bfloat16 [8192, 4096], P('ctx', 'tp')
- relevance_tokens: float32 [8192, 8], P('ctx', 'tp')
Inputs may be any that keep to these rules, and one draw needn't show every extreme that they name: `segment_ids`: ids never fall along the prompt; every document holds 1 to 1024 tokens and one holds exactly 1024.
All inputs are finite; a program needn't handle non-finite values.
Results may differ from a plain program's by a relative error of at most 0.02.
Values may be sent and summed in bfloat16 or wider, within the bound.
A program may use at most 64 MiB of HBM per device.

v0:
```python
import jax
import jax.numpy as jnp
from jax import lax
from jax.sharding import PartitionSpec as P

HEAD_DIM = 128
REACH = 8
KBLK = 512
GROUP = 4
masked_score = -1e30


def passed_along(shard, axis, by):
    count = lax.axis_size(axis)
    pairs = [(i, i + by) for i in range(count) if 0 <= i + by < count]
    return lax.ppermute(shard, axis, pairs)


def masked_scores(query_rows, key_block, row_segment, row_position, key_segment, key_position):
    scores = jnp.einsum(
        "krd,jkd->krj", query_rows, key_block, preferred_element_type=jnp.float32
    ) * HEAD_DIM ** (-0.5)
    visible = (row_segment[:, None] == key_segment[None, :]) & (
        key_position[None, :] <= row_position[:, None]
    )
    return (scores, visible[None])


def to_rows(matrix, tokens, local_groups):
    return (
        matrix.reshape(tokens, local_groups, GROUP, HEAD_DIM)
        .transpose(1, 0, 2, 3)
        .reshape(local_groups, tokens * GROUP, HEAD_DIM)
    )


def on_device(queries, keys, values, w_out, relevance_out, segment_ids):
    tokens = queries.shape[0]
    local_groups = keys.shape[1] // HEAD_DIM
    row_count = tokens * GROUP
    shard_index = lax.axis_index("ctx")
    first_token = shard_index * tokens
    query_rows = to_rows(queries, tokens, local_groups)
    own_segment = lax.dynamic_slice_in_dim(segment_ids, first_token, tokens)
    row_segment = jnp.repeat(own_segment, GROUP)
    row_position = first_token + jnp.repeat(jnp.arange(tokens, dtype=jnp.int32), GROUP)
    earlier = []
    for distance in range(REACH, 0, -1):
        earlier.append(passed_along((keys, values), "ctx", distance))
    window_length = ((REACH + 1) * tokens + KBLK - 1) // KBLK * KBLK
    pad_rows = window_length - (REACH + 1) * tokens
    filler = jnp.zeros((pad_rows, keys.shape[1]), keys.dtype)
    key_window = jnp.concatenate([piece[0] for piece in earlier] + [keys, filler], axis=0)
    value_window = jnp.concatenate([piece[1] for piece in earlier] + [values, filler], axis=0)
    offset = first_token - REACH * tokens
    padded_segments = jnp.concatenate(
        [
            jnp.full((window_length,), -1, jnp.int32),
            segment_ids,
            jnp.full((window_length,), -1, jnp.int32),
        ]
    )
    key_segment = lax.dynamic_slice_in_dim(padded_segments, offset + window_length, window_length)
    key_heads = key_window.reshape(window_length, local_groups, HEAD_DIM)
    value_heads = value_window.reshape(window_length, local_groups, HEAD_DIM)
    doc_start = jnp.sum((segment_ids < own_segment[0]).astype(jnp.int32))
    low_block = (doc_start - offset) // KBLK
    high_block = (first_token + tokens - 1 - offset) // KBLK + 1

    def block_inputs(block):
        start = block * KBLK
        key_block = lax.dynamic_slice_in_dim(key_heads, start, KBLK, 0)
        value_block = lax.dynamic_slice_in_dim(value_heads, start, KBLK, 0)
        segment_block = lax.dynamic_slice_in_dim(key_segment, start, KBLK)
        position_block = offset + start + jnp.arange(KBLK, dtype=jnp.int32)
        scores, visible = masked_scores(
            query_rows, key_block, row_segment, row_position, segment_block, position_block
        )
        return (start, value_block, scores, visible)

    def forward_block(block, carry):
        row_max, total, summed = carry
        start, value_block, scores, visible = block_inputs(block)
        new_max = jnp.maximum(row_max, jnp.max(jnp.where(visible, scores, masked_score), axis=2))
        weights = jnp.where(visible, jnp.exp(scores - new_max[..., None]), 0.0)
        rescale = jnp.exp(row_max - new_max)
        total = total * rescale + jnp.sum(weights, axis=2)
        summed = summed * rescale[..., None] + jnp.einsum(
            "krj,jkd->krd",
            weights.astype(jnp.bfloat16),
            value_block,
            preferred_element_type=jnp.float32,
        )
        return (new_max, total, summed)

    start_carry = (
        jnp.full((local_groups, row_count), masked_score, jnp.float32),
        jnp.zeros((local_groups, row_count), jnp.float32),
        jnp.zeros((local_groups, row_count, HEAD_DIM), jnp.float32),
    )
    row_max, total, summed = lax.fori_loop(low_block, high_block, forward_block, start_carry)
    attention_rows = (summed / total[..., None]).astype(jnp.bfloat16)
    attention = (
        attention_rows.reshape(local_groups, tokens, GROUP, HEAD_DIM)
        .transpose(1, 0, 2, 3)
        .reshape(tokens, local_groups * GROUP * HEAD_DIM)
    )
    totals = lax.psum(jnp.dot(attention, w_out, preferred_element_type=jnp.float32), "tp")
    upper = lax.all_gather(relevance_out, "tp", axis=1, tiled=True).astype(jnp.float32)
    ratio = (upper * totals / (totals * totals + 1.0)).astype(jnp.bfloat16)
    carried_back = lax.dot_general(
        ratio, w_out, (((1,), (1,)), ((), ())), preferred_element_type=jnp.float32
    )
    attention_float = attention.astype(jnp.float32)
    carried = attention_float * carried_back
    relevance_heads = carried.astype(jnp.bfloat16)
    passed = (carried * attention_float / (attention_float * attention_float + 1.0)).astype(
        jnp.bfloat16
    )
    passed_rows = to_rows(passed, tokens, local_groups)

    def backward_block(block, terms):
        start, value_block, scores, visible = block_inputs(block)
        share = jnp.where(visible, jnp.exp(scores - row_max[..., None]), 0.0) / total[..., None]
        inner = jnp.einsum(
            "krd,jkd->krj", passed_rows, value_block, preferred_element_type=jnp.float32
        )
        added = jnp.sum(share * inner, axis=1)
        current = lax.dynamic_slice_in_dim(terms, start, KBLK, 1)
        return lax.dynamic_update_slice_in_dim(terms, current + added, start, 1)

    terms = lax.fori_loop(
        low_block, high_block, backward_block, jnp.zeros((local_groups, window_length), jnp.float32)
    )
    own_terms = lax.dynamic_slice_in_dim(terms, first_token - offset, tokens, 1)
    for distance in range(1, REACH + 1):
        piece = lax.dynamic_slice_in_dim(terms, first_token - distance * tokens - offset, tokens, 1)
        own_terms = own_terms + passed_along(piece, "ctx", -distance)
    return (relevance_heads, own_terms.T)


def solution(mesh):
    placed = (P("ctx", "tp"), P("ctx", "tp"), P("ctx", "tp"), P("tp", None), P("ctx", "tp"), P())
    return jax.shard_map(
        on_device,
        mesh=mesh,
        in_specs=placed,
        out_specs=(P("ctx", "tp"), P("ctx", "tp")),
        check_vma=False,
    )
```

profile of v0, /device:TPU:448, one launch (start us, length us, event | category | flops | bytes accessed | tf_op | source)
XLA Modules:
  0.0 242.1 jit_solution(6290647112543033285)
XLA Ops:
  7.2 1.3 collective-permute-start
  8.5 5.4 %collective-permute-start.1 = (bf16[128,128]{1,0:T(8,128)(2,1)}, bf16[128,128]{1,0:T(8,128)(2,1)S(1)}, u32[]{:S(2)}, u32[]{:S(2)}) collective-permute-start(bf16[128,128]{1,0:T(8,128)(2,1)} %param.11), channel_id=1, source_target_pairs={{0,56},{8,64},{16,72},{24,80},{32,88},{40,96},{48,104},{56,112},{6... | collective-permute-start | bytes 98312 | tf_op jit(solution)/shard_map/ppermute | solution.py:16
  13.9 1.9 collective-permute-start.2
  15.8 1.9 collective-permute-start.3
  17.8 1.9 collective-permute-start.4
  19.7 0.8 dynamic_slice.54
  20.5 1.4 convert_reduce_fusion
  21.9 0.8 fusion.46
  23.4 1.0 reshape_transpose_reshape.9
  24.4 1.9 collective-permute-start.5
  26.3 2.1 collective-permute-start.6
  28.5 1.9 collective-permute-start.7
  30.5 1.3 collective-permute-start.8
  31.8 1.9 collective-permute-start.9
  33.7 1.9 collective-permute-start.10
  35.7 1.9 collective-permute-start.11
  37.7 1.9 collective-permute-start.12
  39.6 0.8 constant_dynamic-update-slice_fusion
  40.4 0.6 collective-permute-done.8
  41.0 3.3 %collective-permute-start.13 = (bf16[128,128]{1,0:T(8,128)(2,1)}, bf16[128,128]{1,0:T(8,128)(2,1)S(1)}, u32[]{:S(2)}, u32[]{:S(2)}) collective-permute-start(bf16[128,128]{1,0:T(8,128)(2,1)} %param.12), channel_id=1, source_target_pairs={{0,24},{8,32},{16,40},{24,48},{32,56},{40,64},{48,72},{56,80},{64,... | collective-permute-start | bytes 98312 | tf_op jit(solution)/shard_map/ppermute | solution.py:16
  44.4 2.9 %collective-permute-start.14 = (bf16[128,128]{1,0:T(8,128)(2,1)}, bf16[128,128]{1,0:T(8,128)(2,1)S(1)}, u32[]{:S(2)}, u32[]{:S(2)}) collective-permute-start(bf16[128,128]{1,0:T(8,128)(2,1)} %param.12), channel_id=1, source_target_pairs={{0,16},{8,24},{16,32},{24,40},{32,48},{40,56},{48,64},{56,72},{64,... | collective-permute-start | bytes 98312 | tf_op jit(solution)/shard_map/ppermute | solution.py:16
  47.3 1.9 collective-permute-start.15
  49.6 3.4 %collective-permute-done.14 = bf16[128,128]{1,0:T(8,128)(2,1)S(1)} collective-permute-done((bf16[128,128]{1,0:T(8,128)(2,1)}, bf16[128,128]{1,0:T(8,128)(2,1)S(1)}, u32[]{:S(2)}, u32[]{:S(2)}) %collective-permute-start.14) | collective-permute-done | bytes 32800 | tf_op jit(solution)/shard_map/ppermute | solution.py:16
  53.0 2.4 %collective-permute-done.15 = bf16[128,128]{1,0:T(8,128)(2,1)S(1)} collective-permute-done((bf16[128,128]{1,0:T(8,128)(2,1)}, bf16[128,128]{1,0:T(8,128)(2,1)S(1)}, u32[]{:S(2)}, u32[]{:S(2)}) %collective-permute-start.15) | collective-permute-done | bytes 32800 | tf_op jit(solution)/shard_map/ppermute | solution.py:16
  55.4 0.8 constant_dynamic-update-slice_fusion.9
  56.3 3.6 %while.26 = (s32[]{:T(128)}, f32[1,512]{1,0:T(1,128)S(1)}, f32[1,512]{1,0:T(1,128)S(1)}, f32[1,512,128]{2,1,0:T(8,128)S(1)}, s32[]{:T(128)}, /*index=5*/s32[1536...) while((s32[]{:T(128)}, f32[1,512]{1,0:T(1,128)S(1)}, ...), condition=%wide.region_4.5_spmd.clone, body=%wide.region_1.4_spmd.clone.sunk | while | flops 139069440 | bytes 4139747 | solution.py:101
  56.7 0.4 select_reduce_fusion.2
  57.4 0.6 fusion.65
  58.5 0.4 select_reduce_fusion.2
  59.3 0.6 fusion.65
  60.2 4.3 %fusion.48 = f32[128,4096]{1,0:T(8,128)} fusion(bf16[128,512]{1,0:T(8,128)(2,1)S(1)} %reshape_transpose_reshape.10, bf16[512,4096]{1,0:T(8,128)(2,1)} %param.13), kind=kOutput, calls=%fused_computation.94 | convolution fusion | flops 536870912 | bytes 6422528 | tf_op jit(solution)/shard_map/dot_general | solution.py:108
  64.5 0.7 all-gather.2.cloned.1.call-update
  65.2 93.4 %all-reduce.2.cloned.1.call-done = f32[128,4096]{1,0:T(8,128)} async-done(((f32[128,4096]{1,0:T(8,128)}), f32[128,4096]{1,0:T(8,128)}) %all-reduce.2.cloned.1.call-update) | async-done | bytes 2097168 | tf_op jit(solution)/shard_map/psum | solution.py:108
  158.6 32.8 %all-gather.2.cloned.1.call-done = bf16[128,4096]{1,0:T(8,128)(2,1)} async-done(((bf16[128,512]{1,0:T(8,128)(2,1)}), bf16[128,4096]{1,0:T(8,128)(2,1)}) %all-gather.2.cloned.1.call-update) | async-done | bytes 1048592 | tf_op jit(solution)/shard_map/all_gather | solution.py:109
  191.4 5.3 %fusion.43 = (bf16[128,512]{1,0:T(8,128)(2,1)S(1)}, bf16[128,512]{1,0:T(8,128)(2,1)}) fusion(bf16[128,512]{1,0:T(8,128)(2,1)S(1)} %reshape_transpose_reshape.10, bf16[512,4096]{1,0:T(8,128)(2,1)} %param.13, f32[128,4096]{1,0:T(8,128)} %all-reduce.2.cloned.1.call-done, bf16[128,4096]{1,0:T(8,128)(2,1)} %all-gather.2.cloned.1.call-done), kind=kOutput, calls=%fused_computation.56 | convolution fusion | flops 540540928 | bytes 7733248 | tf_op jit(solution)/shard_map/dot_general | solution.py:111
  196.8 2.5 %while.27 = (s32[]{:T(128)}, f32[1,1536]{1,0:T(1,128)S(1)}, s32[]{:T(128)}, s32[1536]{0:T(1024)S(1)}, s32[]{:T(128)}, /*index=5*/bf16[1536,1,128]{2,0,1:T(8,128)...) while((s32[]{:T(128)}, f32[1,1536]{1,0:T(1,128)S(1)}, ...), condition=%wide.region_8.9_spmd.clone, body=%wide.region_6.8_spmd.clone.sunk | while | flops 136578048 | bytes 2661103 | solution.py:132
  197.3 0.5 fusion.70
  198.5 0.5 fusion.70
  199.4 5.5 %collective-permute-start.16 = (f32[1,128]{1,0:T(1,128)S(1)}, f32[1,128]{1,0:T(1,128)S(1)}, u32[]{:S(2)}, u32[]{:S(2)}) collective-permute-start(f32[1,128]{1,0:T(1,128)S(1)} %get-tuple-element.257), channel_id=1, source_target_pairs={{8,0},{16,8},{24,16},{32,24},{40,32},{48,40},{56,48},{64,56},{72,6... | collective-permute-start | bytes 1544 | tf_op jit(solution)/shard_map/ppermute | solution.py:16
  204.9 2.7 %collective-permute-start.17 = (f32[1,128]{1,0:T(1,128)S(1)}, f32[1,128]{1,0:T(1,128)S(1)}, u32[]{:S(2)}, u32[]{:S(2)}) collective-permute-start(f32[1,128]{1,0:T(1,128)S(1)} %get-tuple-element.263), channel_id=1, source_target_pairs={{16,0},{24,8},{32,16},{40,24},{48,32},{56,40},{64,48},{72,56},{80,... | collective-permute-start | bytes 1544 | tf_op jit(solution)/shard_map/ppermute | solution.py:16
  207.6 3.6 %collective-permute-start.18 = (f32[1,128]{1,0:T(1,128)S(1)}, f32[1,128]{1,0:T(1,128)S(1)}, u32[]{:S(2)}, u32[]{:S(2)}) collective-permute-start(f32[1,128]{1,0:T(1,128)S(1)} %get-tuple-element.262), channel_id=1, source_target_pairs={{24,0},{32,8},{40,16},{48,24},{56,32},{64,40},{72,48},{80,56},{88,... | collective-permute-start | bytes 1544 | tf_op jit(solution)/shard_map/ppermute | solution.py:16
  211.2 4.5 %collective-permute-start.19 = (f32[1,128]{1,0:T(1,128)S(1)}, f32[1,128]{1,0:T(1,128)S(1)}, u32[]{:S(2)}, u32[]{:S(2)}) collective-permute-start(f32[1,128]{1,0:T(1,128)S(1)} %get-tuple-element.261), channel_id=1, source_target_pairs={{32,0},{40,8},{48,16},{56,24},{64,32},{72,40},{80,48},{88,56},{96,... | collective-permute-start | bytes 1544 | tf_op jit(solution)/shard_map/ppermute | solution.py:16
  215.7 6.3 %collective-permute-start.20 = (f32[1,128]{1,0:T(1,128)S(1)}, f32[1,128]{1,0:T(1,128)S(1)}, u32[]{:S(2)}, u32[]{:S(2)}) collective-permute-start(f32[1,128]{1,0:T(1,128)S(1)} %get-tuple-element.260), channel_id=1, source_target_pairs={{40,0},{48,8},{56,16},{64,24},{72,32},{80,40},{88,48},{96,56},{104... | collective-permute-start | bytes 1544 | tf_op jit(solution)/shard_map/ppermute | solution.py:16
  222.1 5.0 %collective-permute-start.21 = (f32[1,128]{1,0:T(1,128)S(1)}, f32[1,128]{1,0:T(1,128)S(1)}, u32[]{:S(2)}, u32[]{:S(2)}) collective-permute-start(f32[1,128]{1,0:T(1,128)S(1)} %get-tuple-element.259), channel_id=1, source_target_pairs={{48,0},{56,8},{64,16},{72,24},{80,32},{88,40},{96,48},{104,56},{11... | collective-permute-start | bytes 1544 | tf_op jit(solution)/shard_map/ppermute | solution.py:16
  227.1 1.9 collective-permute-start.22
  229.1 1.6 collective-permute-start.23
  230.7 4.0 %collective-permute-done.22 = f32[1,128]{1,0:T(1,128)S(1)} collective-permute-done((f32[1,128]{1,0:T(1,128)S(1)}, f32[1,128]{1,0:T(1,128)S(1)}, u32[]{:S(2)}, u32[]{:S(2)}) %collective-permute-start.22) | collective-permute-done | bytes 544 | tf_op jit(solution)/shard_map/ppermute | solution.py:16
  234.7 0.5 add_bitcast_fusion
  (86 shorter events, 3.9 us)
Async XLA Ops:
  7.2 151.4 %all-reduce.2.cloned.1.call-start = ((), (), s32[]{:S(2)}) async-start(), calls=%async_computation.1 | async-start | bytes 4194304 | tf_op jit(solution)/shard_map/psum | solution.py:108
  7.2 17.2 %collective-permute-start = (bf16[128,128]{1,0:T(8,128)(2,1)}, bf16[128,128]{1,0:T(8,128)(2,1)S(1)}, u32[]{:S(2)}, u32[]{:S(2)}) collective-permute-start(bf16[128,128]{1,0:T(8,128)(2,1)} %param.11), channel_id=1, source_target_pairs={{0,64},{8,72},{16,80},{24,88},{32,96},{40,104},{48,112},{56,120},{... | collective-permute-start | bytes 98312 | tf_op jit(solution)/shard_map/ppermute | solution.py:16
  8.5 17.8 %collective-permute-start.1 = (bf16[128,128]{1,0:T(8,128)(2,1)}, bf16[128,128]{1,0:T(8,128)(2,1)S(1)}, u32[]{:S(2)}, u32[]{:S(2)}) collective-permute-start(bf16[128,128]{1,0:T(8,128)(2,1)} %param.11), channel_id=1, source_target_pairs={{0,56},{8,64},{16,72},{24,80},{32,88},{40,96},{48,104},{56,112},{6... | collective-permute-start | bytes 98312 | tf_op jit(solution)/shard_map/ppermute | solution.py:16
  13.9 14.6 %collective-permute-start.2 = (bf16[128,128]{1,0:T(8,128)(2,1)}, bf16[128,128]{1,0:T(8,128)(2,1)S(1)}, u32[]{:S(2)}, u32[]{:S(2)}) collective-permute-start(bf16[128,128]{1,0:T(8,128)(2,1)} %param.11), channel_id=1, source_target_pairs={{0,48},{8,56},{16,64},{24,72},{32,80},{40,88},{48,96},{56,104},{64... | collective-permute-start | bytes 98312 | tf_op jit(solution)/shard_map/ppermute | solution.py:16
  15.8 14.6 %collective-permute-start.3 = (bf16[128,128]{1,0:T(8,128)(2,1)}, bf16[128,128]{1,0:T(8,128)(2,1)S(1)}, u32[]{:S(2)}, u32[]{:S(2)}) collective-permute-start(bf16[128,128]{1,0:T(8,128)(2,1)} %param.11), channel_id=1, source_target_pairs={{0,40},{8,48},{16,56},{24,64},{32,72},{40,80},{48,88},{56,96},{64,... | collective-permute-start | bytes 98312 | tf_op jit(solution)/shard_map/ppermute | solution.py:16
  17.8 14.0 %collective-permute-start.4 = (bf16[128,128]{1,0:T(8,128)(2,1)}, bf16[128,128]{1,0:T(8,128)(2,1)S(1)}, u32[]{:S(2)}, u32[]{:S(2)}) collective-permute-start(bf16[128,128]{1,0:T(8,128)(2,1)} %param.11), channel_id=1, source_target_pairs={{0,32},{8,40},{16,48},{24,56},{32,64},{40,72},{48,80},{56,88},{64,... | collective-permute-start | bytes 98312 | tf_op jit(solution)/shard_map/ppermute | solution.py:16
  24.4 9.4 %collective-permute-start.5 = (bf16[128,128]{1,0:T(8,128)(2,1)}, bf16[128,128]{1,0:T(8,128)(2,1)S(1)}, u32[]{:S(2)}, u32[]{:S(2)}) collective-permute-start(bf16[128,128]{1,0:T(8,128)(2,1)} %param.11), channel_id=1, source_target_pairs={{0,24},{8,32},{16,40},{24,48},{32,56},{40,64},{48,72},{56,80},{64,... | collective-permute-start | bytes 98312 | tf_op jit(solution)/shard_map/ppermute | solution.py:16
  26.3 9.4 %collective-permute-start.6 = (bf16[128,128]{1,0:T(8,128)(2,1)}, bf16[128,128]{1,0:T(8,128)(2,1)S(1)}, u32[]{:S(2)}, u32[]{:S(2)}) collective-permute-start(bf16[128,128]{1,0:T(8,128)(2,1)} %param.11), channel_id=1, source_target_pairs={{0,16},{8,24},{16,32},{24,40},{32,48},{40,56},{48,64},{56,72},{64,... | collective-permute-start | bytes 98312 | tf_op jit(solution)/shard_map/ppermute | solution.py:16
  28.5 9.2 %collective-permute-start.7 = (bf16[128,128]{1,0:T(8,128)(2,1)}, bf16[128,128]{1,0:T(8,128)(2,1)S(1)}, u32[]{:S(2)}, u32[]{:S(2)}) collective-permute-start(bf16[128,128]{1,0:T(8,128)(2,1)} %param.11), channel_id=1, source_target_pairs={{0,8},{8,16},{16,24},{24,32},{32,40},{40,48},{48,56},{56,64},{64,7... | collective-permute-start | bytes 98312 | tf_op jit(solution)/shard_map/ppermute | solution.py:16
  30.5 10.6 %collective-permute-start.8 = (bf16[128,128]{1,0:T(8,128)(2,1)}, bf16[128,128]{1,0:T(8,128)(2,1)S(1)}, u32[]{:S(2)}, u32[]{:S(2)}) collective-permute-start(bf16[128,128]{1,0:T(8,128)(2,1)} %param.12), channel_id=1, source_target_pairs={{0,64},{8,72},{16,80},{24,88},{32,96},{40,104},{48,112},{56,120},{... | collective-permute-start | bytes 98312 | tf_op jit(solution)/shard_map/ppermute | solution.py:16
  31.8 12.6 %collective-permute-start.9 = (bf16[128,128]{1,0:T(8,128)(2,1)}, bf16[128,128]{1,0:T(8,128)(2,1)S(1)}, u32[]{:S(2)}, u32[]{:S(2)}) collective-permute-start(bf16[128,128]{1,0:T(8,128)(2,1)} %param.12), channel_id=1, source_target_pairs={{0,56},{8,64},{16,72},{24,80},{32,88},{40,96},{48,104},{56,112},{6... | collective-permute-start | bytes 98312 | tf_op jit(solution)/shard_map/ppermute | solution.py:16
  33.7 13.5 %collective-permute-start.10 = (bf16[128,128]{1,0:T(8,128)(2,1)}, bf16[128,128]{1,0:T(8,128)(2,1)S(1)}, u32[]{:S(2)}, u32[]{:S(2)}) collective-permute-start(bf16[128,128]{1,0:T(8,128)(2,1)} %param.12), channel_id=1, source_target_pairs={{0,48},{8,56},{16,64},{24,72},{32,80},{40,88},{48,96},{56,104},{64... | collective-permute-start | bytes 98312 | tf_op jit(solution)/shard_map/ppermute | solution.py:16
  35.7 13.5 %collective-permute-start.11 = (bf16[128,128]{1,0:T(8,128)(2,1)}, bf16[128,128]{1,0:T(8,128)(2,1)S(1)}, u32[]{:S(2)}, u32[]{:S(2)}) collective-permute-start(bf16[128,128]{1,0:T(8,128)(2,1)} %param.12), channel_id=1, source_target_pairs={{0,40},{8,48},{16,56},{24,64},{32,72},{40,80},{48,88},{56,96},{64,... | collective-permute-start | bytes 98312 | tf_op jit(solution)/shard_map/ppermute | solution.py:16
  37.7 11.6 %collective-permute-start.12 = (bf16[128,128]{1,0:T(8,128)(2,1)}, bf16[128,128]{1,0:T(8,128)(2,1)S(1)}, u32[]{:S(2)}, u32[]{:S(2)}) collective-permute-start(bf16[128,128]{1,0:T(8,128)(2,1)} %param.12), channel_id=1, source_target_pairs={{0,32},{8,40},{16,48},{24,56},{32,64},{40,72},{48,80},{56,88},{64,... | collective-permute-start | bytes 98312 | tf_op jit(solution)/shard_map/ppermute | solution.py:16
  41.0 8.6 %collective-permute-start.13 = (bf16[128,128]{1,0:T(8,128)(2,1)}, bf16[128,128]{1,0:T(8,128)(2,1)S(1)}, u32[]{:S(2)}, u32[]{:S(2)}) collective-permute-start(bf16[128,128]{1,0:T(8,128)(2,1)} %param.12), channel_id=1, source_target_pairs={{0,24},{8,32},{16,40},{24,48},{32,56},{40,64},{48,72},{56,80},{64,... | collective-permute-start | bytes 98312 | tf_op jit(solution)/shard_map/ppermute | solution.py:16
  44.4 8.6 %collective-permute-start.14 = (bf16[128,128]{1,0:T(8,128)(2,1)}, bf16[128,128]{1,0:T(8,128)(2,1)S(1)}, u32[]{:S(2)}, u32[]{:S(2)}) collective-permute-start(bf16[128,128]{1,0:T(8,128)(2,1)} %param.12), channel_id=1, source_target_pairs={{0,16},{8,24},{16,32},{24,40},{32,48},{40,56},{48,64},{56,72},{64,... | collective-permute-start | bytes 98312 | tf_op jit(solution)/shard_map/ppermute | solution.py:16
  47.3 8.1 %collective-permute-start.15 = (bf16[128,128]{1,0:T(8,128)(2,1)}, bf16[128,128]{1,0:T(8,128)(2,1)S(1)}, u32[]{:S(2)}, u32[]{:S(2)}) collective-permute-start(bf16[128,128]{1,0:T(8,128)(2,1)} %param.12), channel_id=1, source_target_pairs={{0,8},{8,16},{16,24},{24,32},{32,40},{40,48},{48,56},{56,64},{64,7... | collective-permute-start | bytes 98312 | tf_op jit(solution)/shard_map/ppermute | solution.py:16
  64.4 126.9 %all-gather.2.cloned.1.call-start = ((), (), s32[]{:S(2)}) async-start(), calls=%async_computation | async-start | bytes 1179648 | tf_op jit(solution)/shard_map/all_gather | solution.py:109
  199.4 22.6 %collective-permute-start.16 = (f32[1,128]{1,0:T(1,128)S(1)}, f32[1,128]{1,0:T(1,128)S(1)}, u32[]{:S(2)}, u32[]{:S(2)}) collective-permute-start(f32[1,128]{1,0:T(1,128)S(1)} %get-tuple-element.257), channel_id=1, source_target_pairs={{8,0},{16,8},{24,16},{32,24},{40,32},{48,40},{56,48},{64,56},{72,6... | collective-permute-start | bytes 1544 | tf_op jit(solution)/shard_map/ppermute | solution.py:16
  204.9 22.2 %collective-permute-start.17 = (f32[1,128]{1,0:T(1,128)S(1)}, f32[1,128]{1,0:T(1,128)S(1)}, u32[]{:S(2)}, u32[]{:S(2)}) collective-permute-start(f32[1,128]{1,0:T(1,128)S(1)} %get-tuple-element.263), channel_id=1, source_target_pairs={{16,0},{24,8},{32,16},{40,24},{48,32},{56,40},{64,48},{72,56},{80,... | collective-permute-start | bytes 1544 | tf_op jit(solution)/shard_map/ppermute | solution.py:16
  207.6 21.5 %collective-permute-start.18 = (f32[1,128]{1,0:T(1,128)S(1)}, f32[1,128]{1,0:T(1,128)S(1)}, u32[]{:S(2)}, u32[]{:S(2)}) collective-permute-start(f32[1,128]{1,0:T(1,128)S(1)} %get-tuple-element.262), channel_id=1, source_target_pairs={{24,0},{32,8},{40,16},{48,24},{56,32},{64,40},{72,48},{80,56},{88,... | collective-permute-start | bytes 1544 | tf_op jit(solution)/shard_map/ppermute | solution.py:16
  211.2 19.4 %collective-permute-start.19 = (f32[1,128]{1,0:T(1,128)S(1)}, f32[1,128]{1,0:T(1,128)S(1)}, u32[]{:S(2)}, u32[]{:S(2)}) collective-permute-start(f32[1,128]{1,0:T(1,128)S(1)} %get-tuple-element.261), channel_id=1, source_target_pairs={{32,0},{40,8},{48,16},{56,24},{64,32},{72,40},{80,48},{88,56},{96,... | collective-permute-start | bytes 1544 | tf_op jit(solution)/shard_map/ppermute | solution.py:16
  215.7 15.0 %collective-permute-start.20 = (f32[1,128]{1,0:T(1,128)S(1)}, f32[1,128]{1,0:T(1,128)S(1)}, u32[]{:S(2)}, u32[]{:S(2)}) collective-permute-start(f32[1,128]{1,0:T(1,128)S(1)} %get-tuple-element.260), channel_id=1, source_target_pairs={{40,0},{48,8},{56,16},{64,24},{72,32},{80,40},{88,48},{96,56},{104... | collective-permute-start | bytes 1544 | tf_op jit(solution)/shard_map/ppermute | solution.py:16
  222.1 8.6 %collective-permute-start.21 = (f32[1,128]{1,0:T(1,128)S(1)}, f32[1,128]{1,0:T(1,128)S(1)}, u32[]{:S(2)}, u32[]{:S(2)}) collective-permute-start(f32[1,128]{1,0:T(1,128)S(1)} %get-tuple-element.259), channel_id=1, source_target_pairs={{48,0},{56,8},{64,16},{72,24},{80,32},{88,40},{96,48},{104,56},{11... | collective-permute-start | bytes 1544 | tf_op jit(solution)/shard_map/ppermute | solution.py:16
  227.1 7.6 %collective-permute-start.22 = (f32[1,128]{1,0:T(1,128)S(1)}, f32[1,128]{1,0:T(1,128)S(1)}, u32[]{:S(2)}, u32[]{:S(2)}) collective-permute-start(f32[1,128]{1,0:T(1,128)S(1)} %get-tuple-element.258), channel_id=1, source_target_pairs={{56,0},{64,8},{72,16},{80,24},{88,32},{96,40},{104,48},{112,56},{1... | collective-permute-start | bytes 1544 | tf_op jit(solution)/shard_map/ppermute | solution.py:16
  229.1 5.6 %collective-permute-start.23 = (f32[1,128]{1,0:T(1,128)S(1)}, f32[1,128]{1,0:T(1,128)S(1)}, u32[]{:S(2)}, u32[]{:S(2)}) collective-permute-start(f32[1,128]{1,0:T(1,128)S(1)} %get-tuple-element.264), channel_id=1, source_target_pairs={{64,0},{72,8},{80,16},{88,24},{96,32},{104,40},{112,48},{120,56},{... | collective-permute-start | bytes 1544 | tf_op jit(solution)/shard_map/ppermute | solution.py:16
Sparse Core Ops, SparseCore 0:
  64.6 93.9 all-reduce.1
  160.7 30.5 all-gather.1
where the time goes:
time: 243 us; the launch traced here: 242 us
  waiting for transfers between devices  138 us (57%)
  starting transfers between devices  66.8 us (27%)
  between operations  15.3 us (6%)
  matrix products  13.3 us (5%)
  local copies, waits for them, and re-layouts  5.22 us (2%)
  other arithmetic  3.65 us (2%)
    psum x1, waiting for transfers between devices, on_device(): lax.psum(jnp.dot(attention, w_out, preferred_element_type=jnp.float32), '...  93.4 us
    ppermute x24, starting transfers between devices, passed_along(): return lax.ppermute(shard, axis, pairs)  66.7 us
    all_gather x1, waiting for transfers between devices, on_device(): lax.all_gather(relevance_out, 'tp', axis=1, tiled=True).astype(jnp.float32)  32.8 us
    ppermute x24, waiting for transfers between devices, passed_along(): return lax.ppermute(shard, axis, pairs)  10.8 us
    dot_general x1, matrix products, on_device(): lax.dot_general(ratio, w_out, (((1,), (1,)), ((), ())), preferred_element...  5.35 us
  transfers between devices with their start and end apart: 26, of which 7 were waited for; matrix products, arithmetic and copies ran while one was open for 2% of the time, Pallas kernels for 0%

commit v1 on v0

--- a/solution.py
+++ b/solution.py
@@ -8,6 +8,13 @@
 KBLK = 512
 GROUP = 4
 masked_score = -1e30
+
+
+def all_by_exchange(array, axis, along):
+    devices = lax.axis_size(axis)
+    parts = jnp.stack([array for _ in range(devices)])
+    parts = lax.all_to_all(parts, axis, split_axis=0, concat_axis=0)
+    return jnp.concatenate(parts, axis=along)
 
 
 def passed_along(shard, axis, by):
@@ -106,7 +113,7 @@
         .reshape(tokens, local_groups * GROUP * HEAD_DIM)
     )
     totals = lax.psum(jnp.dot(attention, w_out, preferred_element_type=jnp.float32), "tp")
-    upper = lax.all_gather(relevance_out, "tp", axis=1, tiled=True).astype(jnp.float32)
+    upper = all_by_exchange(relevance_out, "tp", 1).astype(jnp.float32)
     ratio = (upper * totals / (totals * totals + 1.0)).astype(jnp.bfloat16)
     carried_back = lax.dot_general(
         ratio, w_out, (((1,), (1,)), ((), ())), preferred_element_type=jnp.float32

time: 243 us -> 215 us (0.88)
  waiting for transfers between devices: 138 us -> 105 us
  starting transfers between devices: 66.8 us -> 72 us
    all_gather x1 -> x0, waiting for transfers between devices: 32.8 us -> none  [on_device(): lax.all_gather(relevance_out, 'tp', axis=1, tiled=True).astype(jnp.float32)]
    all_to_all x0 -> x1, starting transfers between devices: none -> 4.3 us  [all_by_exchange(): parts = lax.all_to_all(parts, axis, split_axis=0, concat_axis=0)]
  transfers between devices with their start and end apart: 26 -> 26, of which waited for: 7 -> 6; matrix products, arithmetic and copies ran while one was open for 2% -> 5% of each run, Pallas kernels for 0% -> 0%
where the time goes in v1:
time: 215 us
  waiting for transfers between devices  105 us (49%)
  starting transfers between devices  72 us (33%)
  between operations  15.4 us (7%)
  matrix products  14.9 us (7%)
  local copies, waits for them, and re-layouts  4.99 us (2%)
  other arithmetic  2.46 us (1%)
    psum x1, waiting for transfers between devices, on_device(): lax.psum(jnp.dot(attention, w_out, preferred_element_type=jnp.float32), '...  93.8 us
    ppermute x24, starting transfers between devices, passed_along(): return lax.ppermute(shard, axis, pairs)  67.7 us
    ppermute x24, waiting for transfers between devices, passed_along(): return lax.ppermute(shard, axis, pairs)  10.8 us
    dot_general x1, matrix products, on_device(): lax.dot_general(ratio, w_out, (((1,), (1,)), ((), ())), preferred_element...  5.05 us
    dot_general x1, matrix products, on_device(): jnp.dot(attention, w_out, preferred_element_type=jnp.float32)  4.32 us
    all_to_all x1, starting transfers between devices, all_by_exchange(): parts = lax.all_to_all(parts, axis, split_axis=0, concat_axis=0)  4.3 us
  transfers between devices with their start and end apart: 26, of which 6 were waited for; matrix products, arithmetic and copies ran while one was open for 5% of the time, Pallas kernels for 0%

profile of v1, /device:TPU:448, one launch (start us, length us, event | category | flops | bytes accessed | tf_op | source)
XLA Modules:
  0.0 214.5 jit_solution(11622115641869812324)
XLA Ops:
  7.2 1.4 collective-permute-start
  8.6 5.4 %collective-permute-start.1 = (bf16[128,128]{1,0:T(8,128)(2,1)}, bf16[128,128]{1,0:T(8,128)(2,1)S(1)}, u32[]{:S(2)}, u32[]{:S(2)}) collective-permute-start(bf16[128,128]{1,0:T(8,128)(2,1)} %param.11), channel_id=1, source_target_pairs={{0,56},{8,64},{16,72},{24,80},{32,88},{40,96},{48,104},{56,112},{6... | collective-permute-start | bytes 98312 | tf_op jit(solution)/shard_map/ppermute | solution.py:23
  14.0 1.9 collective-permute-start.2
  15.9 1.9 collective-permute-start.3
  17.9 1.9 collective-permute-start.4
  19.8 2.0 stack.2
  21.8 4.3 %all-to-all-start = ((bf16[8,128,512]{2,1,0:T(8,128)(2,1)}), bf16[8,128,512]{2,1,0:T(8,128)(2,1)S(1)}, u32[]{:S(2)}, u32[]{:S(2)}) async-start(bf16[8,128,512]{2,1,0:T(8,128)(2,1)} %stack.2), calls=%async_computation | async-start | bytes 2097152 | tf_op jit(solution)/shard_map/all_to_all | solution.py:16
  26.3 0.7 convert_reduce_fusion
  27.8 1.9 collective-permute-start.5
  29.8 2.1 collective-permute-start.6
  31.9 1.9 collective-permute-start.7
  33.9 1.3 collective-permute-start.8
  35.3 1.9 collective-permute-start.9
  37.2 1.9 collective-permute-start.10
  39.2 1.9 collective-permute-start.11
  41.1 1.9 collective-permute-start.12
  43.1 0.8 collective-permute-done.8
  43.9 3.3 %collective-permute-start.13 = (bf16[128,128]{1,0:T(8,128)(2,1)S(1)}, bf16[128,128]{1,0:T(8,128)(2,1)S(1)}, u32[]{:S(2)}, u32[]{:S(2)}) collective-permute-start(bf16[128,128]{1,0:T(8,128)(2,1)S(1)} %copy-done.9), channel_id=1, source_target_pairs={{0,24},{8,32},{16,40},{24,48},{32,56},{40,64},{48,72},{56,80},{64,... | collective-permute-start | bytes 98312 | tf_op jit(solution)/shard_map/ppermute | solution.py:23
  47.3 2.8 %collective-permute-start.14 = (bf16[128,128]{1,0:T(8,128)(2,1)S(1)}, bf16[128,128]{1,0:T(8,128)(2,1)S(1)}, u32[]{:S(2)}, u32[]{:S(2)}) collective-permute-start(bf16[128,128]{1,0:T(8,128)(2,1)S(1)} %copy-done.9), channel_id=1, source_target_pairs={{0,16},{8,24},{16,32},{24,40},{32,48},{40,56},{48,64},{56,72},{64,... | collective-permute-start | bytes 98312 | tf_op jit(solution)/shard_map/ppermute | solution.py:23
  50.2 1.9 collective-permute-start.15
  52.2 0.4 collective-permute-done.13
  52.5 3.4 %collective-permute-done.14 = bf16[128,128]{1,0:T(8,128)(2,1)S(1)} collective-permute-done((bf16[128,128]{1,0:T(8,128)(2,1)S(1)}, bf16[128,128]{1,0:T(8,128)(2,1)S(1)}, u32[]{:S(2)}, u32[]{:S(2)}) %collective-permute-start.14) | collective-permute-done | bytes 32800 | tf_op jit(solution)/shard_map/ppermute | solution.py:23
  55.9 2.2 %collective-permute-done.15 = bf16[128,128]{1,0:T(8,128)(2,1)S(1)} collective-permute-done((bf16[128,128]{1,0:T(8,128)(2,1)S(1)}, bf16[128,128]{1,0:T(8,128)(2,1)S(1)}, u32[]{:S(2)}, u32[]{:S(2)}) %collective-permute-start.15) | collective-permute-done | bytes 32800 | tf_op jit(solution)/shard_map/ppermute | solution.py:23
  58.2 3.6 %while.26 = (s32[]{:T(128)}, f32[1,512]{1,0:T(1,128)S(1)}, f32[1,512]{1,0:T(1,128)S(1)}, f32[1,512,128]{2,1,0:T(8,128)S(1)}, s32[]{:T(128)}, /*index=5*/s32[1536...) while((s32[]{:T(128)}, f32[1,512]{1,0:T(1,128)S(1)}, ...), condition=%wide.region_4.5_spmd.clone, body=%wide.region_1.4_spmd.clone.sunk | while | flops 139069440 | bytes 4139747 | solution.py:108
  58.6 0.4 select_reduce_fusion.2
  59.0 0.3 fusion.64
  59.3 0.6 fusion.65
  60.4 0.4 select_reduce_fusion.2
  61.1 0.6 fusion.65
  61.8 0.6 copy-done.3
  62.7 4.3 %fusion.48 = f32[128,4096]{1,0:T(8,128)} fusion(bf16[128,512]{1,0:T(8,128)(2,1)S(1)} %reshape_transpose_reshape.10, bf16[512,4096]{1,0:T(8,128)(2,1)} %param.13), kind=kOutput, calls=%fused_computation.95 | convolution fusion | flops 536870912 | bytes 6422528 | tf_op jit(solution)/shard_map/dot_general | solution.py:115
  67.6 93.8 %all-reduce.2.cloned.1.call-done = f32[128,4096]{1,0:T(8,128)} async-done(((f32[128,4096]{1,0:T(8,128)}), f32[128,4096]{1,0:T(8,128)}) %all-reduce.2.cloned.1.call-update) | async-done | bytes 2097168 | tf_op jit(solution)/shard_map/psum | solution.py:115
  161.4 5.0 %fusion.43 = (bf16[128,512]{1,0:T(8,128)(2,1)S(1)}, bf16[128,512]{1,0:T(8,128)(2,1)}) fusion(bf16[128,512]{1,0:T(8,128)(2,1)S(1)} %copy-done.1, bf16[512,4096]{1,0:T(8,128)(2,1)} %param.13, f32[128,4096]{1,0:T(8,128)} %all-reduce.2.cloned.1.call-done, f32[128,4096]{1,0:T(8,128)S(1)} %bitcast.98), kind=kOutput, calls=%fused_computation.57 | convolution fusion | flops 540016640 | bytes 8781824 | tf_op jit(solution)/shard_map/dot_general | solution.py:118
  166.6 4.4 %while.27 = (s32[]{:T(128)}, f32[1,1536]{1,0:T(1,128)S(1)}, s32[]{:T(128)}, s32[1536]{0:T(1024)S(1)}, s32[]{:T(128)}, /*index=5*/bf16[1536,1,128]{2,0,1:T(8,128)...) while((s32[]{:T(128)}, f32[1,1536]{1,0:T(1,128)S(1)}, ...), condition=%wide.region_8.9_spmd.clone, body=%wide.region_6.8_spmd.clone.sunk | while | flops 136578048 | bytes 2661103 | solution.py:139
  167.0 1.4 fusion.70
  168.4 0.3 fusion.71
  169.2 1.4 fusion.70
  170.6 0.3 fusion.71
  171.0 5.5 %collective-permute-start.16 = (f32[1,128]{1,0:T(1,128)S(1)}, f32[1,128]{1,0:T(1,128)S(1)}, u32[]{:S(2)}, u32[]{:S(2)}) collective-permute-start(f32[1,128]{1,0:T(1,128)S(1)} %get-tuple-element.257), channel_id=1, source_target_pairs={{8,0},{16,8},{24,16},{32,24},{40,32},{48,40},{56,48},{64,56},{72,6... | collective-permute-start | bytes 1544 | tf_op jit(solution)/shard_map/ppermute | solution.py:23
  176.5 2.7 %collective-permute-start.17 = (f32[1,128]{1,0:T(1,128)S(1)}, f32[1,128]{1,0:T(1,128)S(1)}, u32[]{:S(2)}, u32[]{:S(2)}) collective-permute-start(f32[1,128]{1,0:T(1,128)S(1)} %get-tuple-element.263), channel_id=1, source_target_pairs={{16,0},{24,8},{32,16},{40,24},{48,32},{56,40},{64,48},{72,56},{80,... | collective-permute-start | bytes 1544 | tf_op jit(solution)/shard_map/ppermute | solution.py:23
  179.2 3.6 %collective-permute-start.18 = (f32[1,128]{1,0:T(1,128)S(1)}, f32[1,128]{1,0:T(1,128)S(1)}, u32[]{:S(2)}, u32[]{:S(2)}) collective-permute-start(f32[1,128]{1,0:T(1,128)S(1)} %get-tuple-element.262), channel_id=1, source_target_pairs={{24,0},{32,8},{40,16},{48,24},{56,32},{64,40},{72,48},{80,56},{88,... | collective-permute-start | bytes 1544 | tf_op jit(solution)/shard_map/ppermute | solution.py:23
  182.8 4.5 %collective-permute-start.19 = (f32[1,128]{1,0:T(1,128)S(1)}, f32[1,128]{1,0:T(1,128)S(1)}, u32[]{:S(2)}, u32[]{:S(2)}) collective-permute-start(f32[1,128]{1,0:T(1,128)S(1)} %get-tuple-element.261), channel_id=1, source_target_pairs={{32,0},{40,8},{48,16},{56,24},{64,32},{72,40},{80,48},{88,56},{96,... | collective-permute-start | bytes 1544 | tf_op jit(solution)/shard_map/ppermute | solution.py:23
  187.3 7.2 %collective-permute-start.20 = (f32[1,128]{1,0:T(1,128)S(1)}, f32[1,128]{1,0:T(1,128)S(1)}, u32[]{:S(2)}, u32[]{:S(2)}) collective-permute-start(f32[1,128]{1,0:T(1,128)S(1)} %get-tuple-element.260), channel_id=1, source_target_pairs={{40,0},{48,8},{56,16},{64,24},{72,32},{80,40},{88,48},{96,56},{104... | collective-permute-start | bytes 1544 | tf_op jit(solution)/shard_map/ppermute | solution.py:23
  194.6 5.0 %collective-permute-start.21 = (f32[1,128]{1,0:T(1,128)S(1)}, f32[1,128]{1,0:T(1,128)S(1)}, u32[]{:S(2)}, u32[]{:S(2)}) collective-permute-start(f32[1,128]{1,0:T(1,128)S(1)} %get-tuple-element.259), channel_id=1, source_target_pairs={{48,0},{56,8},{64,16},{72,24},{80,32},{88,40},{96,48},{104,56},{11... | collective-permute-start | bytes 1544 | tf_op jit(solution)/shard_map/ppermute | solution.py:23
  199.6 1.9 collective-permute-start.22
  201.5 1.6 collective-permute-start.23
  203.2 4.0 %collective-permute-done.22 = f32[1,128]{1,0:T(1,128)S(1)} collective-permute-done((f32[1,128]{1,0:T(1,128)S(1)}, f32[1,128]{1,0:T(1,128)S(1)}, u32[]{:S(2)}, u32[]{:S(2)}) %collective-permute-start.22) | collective-permute-done | bytes 544 | tf_op jit(solution)/shard_map/ppermute | solution.py:23
  207.2 0.5 add_bitcast_fusion
  (110 shorter events, 3.4 us)
Async XLA Ops:
  7.2 20.7 %copy-start.8 = (bf16[128,128]{1,0:T(8,128)(2,1)S(1)}, bf16[128,128]{1,0:T(8,128)(2,1)}, u32[]{:S(2)}) copy-start(bf16[128,128]{1,0:T(8,128)(2,1)} %param.11) | copy-start | bytes 98308
  7.2 19.0 %copy-start.5 = (s32[8192]{0:T(1024)S(1)}, s32[8192]{0:T(1024)}, u32[]{:S(2)}) copy-start(s32[8192]{0:T(1024)} %param.15) | copy-start | bytes 98308
  7.2 20.5 %copy-start.2 = (bf16[128,512]{1,0:T(8,128)(2,1)S(1)}, bf16[128,512]{1,0:T(8,128)(2,1)}, u32[]{:S(2)}) copy-start(bf16[128,512]{1,0:T(8,128)(2,1)} %param.10) | copy-start | bytes 393220
  7.2 26.7 %copy-start.9 = (bf16[128,128]{1,0:T(8,128)(2,1)S(1)}, bf16[128,128]{1,0:T(8,128)(2,1)}, u32[]{:S(2)}) copy-start(bf16[128,128]{1,0:T(8,128)(2,1)} %param.12) | copy-start | bytes 98308
  7.2 20.6 %collective-permute-start = (bf16[128,128]{1,0:T(8,128)(2,1)}, bf16[128,128]{1,0:T(8,128)(2,1)S(1)}, u32[]{:S(2)}, u32[]{:S(2)}) collective-permute-start(bf16[128,128]{1,0:T(8,128)(2,1)} %param.11), channel_id=1, source_target_pairs={{0,64},{8,72},{16,80},{24,88},{32,96},{40,104},{48,112},{56,120},{... | collective-permute-start | bytes 98312 | tf_op jit(solution)/shard_map/ppermute | solution.py:23
  8.6 21.2 %collective-permute-start.1 = (bf16[128,128]{1,0:T(8,128)(2,1)}, bf16[128,128]{1,0:T(8,128)(2,1)S(1)}, u32[]{:S(2)}, u32[]{:S(2)}) collective-permute-start(bf16[128,128]{1,0:T(8,128)(2,1)} %param.11), channel_id=1, source_target_pairs={{0,56},{8,64},{16,72},{24,80},{32,88},{40,96},{48,104},{56,112},{6... | collective-permute-start | bytes 98312 | tf_op jit(solution)/shard_map/ppermute | solution.py:23
  14.0 17.9 %collective-permute-start.2 = (bf16[128,128]{1,0:T(8,128)(2,1)}, bf16[128,128]{1,0:T(8,128)(2,1)S(1)}, u32[]{:S(2)}, u32[]{:S(2)}) collective-permute-start(bf16[128,128]{1,0:T(8,128)(2,1)} %param.11), channel_id=1, source_target_pairs={{0,48},{8,56},{16,64},{24,72},{32,80},{40,88},{48,96},{56,104},{64... | collective-permute-start | bytes 98312 | tf_op jit(solution)/shard_map/ppermute | solution.py:23
  15.9 18.0 %collective-permute-start.3 = (bf16[128,128]{1,0:T(8,128)(2,1)}, bf16[128,128]{1,0:T(8,128)(2,1)S(1)}, u32[]{:S(2)}, u32[]{:S(2)}) collective-permute-start(bf16[128,128]{1,0:T(8,128)(2,1)} %param.11), channel_id=1, source_target_pairs={{0,40},{8,48},{16,56},{24,64},{32,72},{40,80},{48,88},{56,96},{64,... | collective-permute-start | bytes 98312 | tf_op jit(solution)/shard_map/ppermute | solution.py:23
  17.9 17.4 %collective-permute-start.4 = (bf16[128,128]{1,0:T(8,128)(2,1)}, bf16[128,128]{1,0:T(8,128)(2,1)S(1)}, u32[]{:S(2)}, u32[]{:S(2)}) collective-permute-start(bf16[128,128]{1,0:T(8,128)(2,1)} %param.11), channel_id=1, source_target_pairs={{0,32},{8,40},{16,48},{24,56},{32,64},{40,72},{48,80},{56,88},{64,... | collective-permute-start | bytes 98312 | tf_op jit(solution)/shard_map/ppermute | solution.py:23
  21.8 45.3 %all-to-all-start = ((bf16[8,128,512]{2,1,0:T(8,128)(2,1)}), bf16[8,128,512]{2,1,0:T(8,128)(2,1)S(1)}, u32[]{:S(2)}, u32[]{:S(2)}) async-start(bf16[8,128,512]{2,1,0:T(8,128)(2,1)} %stack.2), calls=%async_computation | async-start | bytes 2097152 | tf_op jit(solution)/shard_map/all_to_all | solution.py:16
  26.1 135.3 %all-reduce.2.cloned.1.call-start = ((), (), s32[]{:S(2)}) async-start(), calls=%async_computation.1 | async-start | bytes 4194304 | tf_op jit(solution)/shard_map/psum | solution.py:115
  27.8 9.4 %collective-permute-start.5 = (bf16[128,128]{1,0:T(8,128)(2,1)S(1)}, bf16[128,128]{1,0:T(8,128)(2,1)S(1)}, u32[]{:S(2)}, u32[]{:S(2)}) collective-permute-start(bf16[128,128]{1,0:T(8,128)(2,1)S(1)} %copy-done.8), channel_id=1, source_target_pairs={{0,24},{8,32},{16,40},{24,48},{32,56},{40,64},{48,72},{56,80},{64,... | collective-permute-start | bytes 98312 | tf_op jit(solution)/shard_map/ppermute | solution.py:23
  29.8 9.4 %collective-permute-start.6 = (bf16[128,128]{1,0:T(8,128)(2,1)S(1)}, bf16[128,128]{1,0:T(8,128)(2,1)S(1)}, u32[]{:S(2)}, u32[]{:S(2)}) collective-permute-start(bf16[128,128]{1,0:T(8,128)(2,1)S(1)} %copy-done.8), channel_id=1, source_target_pairs={{0,16},{8,24},{16,32},{24,40},{32,48},{40,56},{48,64},{56,72},{64,... | collective-permute-start | bytes 98312 | tf_op jit(solution)/shard_map/ppermute | solution.py:23
  31.9 9.2 %collective-permute-start.7 = (bf16[128,128]{1,0:T(8,128)(2,1)S(1)}, bf16[128,128]{1,0:T(8,128)(2,1)S(1)}, u32[]{:S(2)}, u32[]{:S(2)}) collective-permute-start(bf16[128,128]{1,0:T(8,128)(2,1)S(1)} %copy-done.8), channel_id=1, source_target_pairs={{0,8},{8,16},{16,24},{24,32},{32,40},{40,48},{48,56},{56,64},{64,7... | collective-permute-start | bytes 98312 | tf_op jit(solution)/shard_map/ppermute | solution.py:23
  33.9 10.0 %collective-permute-start.8 = (bf16[128,128]{1,0:T(8,128)(2,1)S(1)}, bf16[128,128]{1,0:T(8,128)(2,1)S(1)}, u32[]{:S(2)}, u32[]{:S(2)}) collective-permute-start(bf16[128,128]{1,0:T(8,128)(2,1)S(1)} %copy-done.9), channel_id=1, source_target_pairs={{0,64},{8,72},{16,80},{24,88},{32,96},{40,104},{48,112},{56,120},{... | collective-permute-start | bytes 98312 | tf_op jit(solution)/shard_map/ppermute | solution.py:23
  35.3 12.0 %collective-permute-start.9 = (bf16[128,128]{1,0:T(8,128)(2,1)S(1)}, bf16[128,128]{1,0:T(8,128)(2,1)S(1)}, u32[]{:S(2)}, u32[]{:S(2)}) collective-permute-start(bf16[128,128]{1,0:T(8,128)(2,1)S(1)} %copy-done.9), channel_id=1, source_target_pairs={{0,56},{8,64},{16,72},{24,80},{32,88},{40,96},{48,104},{56,112},{6... | collective-permute-start | bytes 98312 | tf_op jit(solution)/shard_map/ppermute | solution.py:23
  37.2 12.9 %collective-permute-start.10 = (bf16[128,128]{1,0:T(8,128)(2,1)S(1)}, bf16[128,128]{1,0:T(8,128)(2,1)S(1)}, u32[]{:S(2)}, u32[]{:S(2)}) collective-permute-start(bf16[128,128]{1,0:T(8,128)(2,1)S(1)} %copy-done.9), channel_id=1, source_target_pairs={{0,48},{8,56},{16,64},{24,72},{32,80},{40,88},{48,96},{56,104},{64... | collective-permute-start | bytes 98312 | tf_op jit(solution)/shard_map/ppermute | solution.py:23
  39.2 12.9 %collective-permute-start.11 = (bf16[128,128]{1,0:T(8,128)(2,1)S(1)}, bf16[128,128]{1,0:T(8,128)(2,1)S(1)}, u32[]{:S(2)}, u32[]{:S(2)}) collective-permute-start(bf16[128,128]{1,0:T(8,128)(2,1)S(1)} %copy-done.9), channel_id=1, source_target_pairs={{0,40},{8,48},{16,56},{24,64},{32,72},{40,80},{48,88},{56,96},{64,... | collective-permute-start | bytes 98312 | tf_op jit(solution)/shard_map/ppermute | solution.py:23
  41.1 11.0 %collective-permute-start.12 = (bf16[128,128]{1,0:T(8,128)(2,1)S(1)}, bf16[128,128]{1,0:T(8,128)(2,1)S(1)}, u32[]{:S(2)}, u32[]{:S(2)}) collective-permute-start(bf16[128,128]{1,0:T(8,128)(2,1)S(1)} %copy-done.9), channel_id=1, source_target_pairs={{0,32},{8,40},{16,48},{24,56},{32,64},{40,72},{48,80},{56,88},{64,... | collective-permute-start | bytes 98312 | tf_op jit(solution)/shard_map/ppermute | solution.py:23
  43.9 8.6 %collective-permute-start.13 = (bf16[128,128]{1,0:T(8,128)(2,1)S(1)}, bf16[128,128]{1,0:T(8,128)(2,1)S(1)}, u32[]{:S(2)}, u32[]{:S(2)}) collective-permute-start(bf16[128,128]{1,0:T(8,128)(2,1)S(1)} %copy-done.9), channel_id=1, source_target_pairs={{0,24},{8,32},{16,40},{24,48},{32,56},{40,64},{48,72},{56,80},{64,... | collective-permute-start | bytes 98312 | tf_op jit(solution)/shard_map/ppermute | solution.py:23
  47.3 8.6 %collective-permute-start.14 = (bf16[128,128]{1,0:T(8,128)(2,1)S(1)}, bf16[128,128]{1,0:T(8,128)(2,1)S(1)}, u32[]{:S(2)}, u32[]{:S(2)}) collective-permute-start(bf16[128,128]{1,0:T(8,128)(2,1)S(1)} %copy-done.9), channel_id=1, source_target_pairs={{0,16},{8,24},{16,32},{24,40},{32,48},{40,56},{48,64},{56,72},{64,... | collective-permute-start | bytes 98312 | tf_op jit(solution)/shard_map/ppermute | solution.py:23
  50.2 7.9 %collective-permute-start.15 = (bf16[128,128]{1,0:T(8,128)(2,1)S(1)}, bf16[128,128]{1,0:T(8,128)(2,1)S(1)}, u32[]{:S(2)}, u32[]{:S(2)}) collective-permute-start(bf16[128,128]{1,0:T(8,128)(2,1)S(1)} %copy-done.9), channel_id=1, source_target_pairs={{0,8},{8,16},{16,24},{24,32},{32,40},{40,48},{48,56},{56,64},{64,7... | collective-permute-start | bytes 98312 | tf_op jit(solution)/shard_map/ppermute | solution.py:23
  61.8 0.7 copy-start.3
  61.8 5.2 %copy-start.6 = (s32[128]{0:T(128)}, s32[128]{0:T(128)S(1)}, u32[]{:S(2)}) copy-start(s32[128]{0:T(128)S(1)} %get-tuple-element.534) | copy-start | bytes 1540
  61.8 5.2 %copy-start.10 = (bf16[1536,1,128]{2,0,1:T(8,128)(2,1)}, bf16[1536,1,128]{2,0,1:T(8,128)(2,1)S(1)}, u32[]{:S(2)}) copy-start(bf16[1536,1,128]{2,0,1:T(8,128)(2,1)S(1)} %get-tuple-element.567) | copy-start | bytes 1179652
  62.7 4.3 %copy-start = (bf16[128,512]{1,0:T(8,128)(2,1)}, bf16[128,512]{1,0:T(8,128)(2,1)S(1)}, u32[]{:S(2)}) copy-start(bf16[128,512]{1,0:T(8,128)(2,1)S(1)} %reshape_transpose_reshape.10) | copy-start | bytes 393220
  67.4 94.0 %copy-start.1 = (bf16[128,512]{1,0:T(8,128)(2,1)S(1)}, bf16[128,512]{1,0:T(8,128)(2,1)}, u32[]{:S(2)}) copy-start(bf16[128,512]{1,0:T(8,128)(2,1)} %copy-done) | copy-start | bytes 393220
  161.4 5.2 %copy-start.4 = (bf16[1,512,128]{2,1,0:T(8,128)(2,1)S(1)}, bf16[1,512,128]{2,1,0:T(8,128)(2,1)}, u32[]{:S(2)}) copy-start(bf16[1,512,128]{2,1,0:T(8,128)(2,1)} %copy-done.3) | copy-start | bytes 393220
  161.4 5.2 %copy-start.7 = (s32[128]{0:T(128)S(1)}, s32[128]{0:T(128)}, u32[]{:S(2)}) copy-start(s32[128]{0:T(128)} %copy-done.6) | copy-start | bytes 1540
  171.0 23.5 %collective-permute-start.16 = (f32[1,128]{1,0:T(1,128)S(1)}, f32[1,128]{1,0:T(1,128)S(1)}, u32[]{:S(2)}, u32[]{:S(2)}) collective-permute-start(f32[1,128]{1,0:T(1,128)S(1)} %get-tuple-element.257), channel_id=1, source_target_pairs={{8,0},{16,8},{24,16},{32,24},{40,32},{48,40},{56,48},{64,56},{72,6... | collective-permute-start | bytes 1544 | tf_op jit(solution)/shard_map/ppermute | solution.py:23
  176.5 23.1 %collective-permute-start.17 = (f32[1,128]{1,0:T(1,128)S(1)}, f32[1,128]{1,0:T(1,128)S(1)}, u32[]{:S(2)}, u32[]{:S(2)}) collective-permute-start(f32[1,128]{1,0:T(1,128)S(1)} %get-tuple-element.263), channel_id=1, source_target_pairs={{16,0},{24,8},{32,16},{40,24},{48,32},{56,40},{64,48},{72,56},{80,... | collective-permute-start | bytes 1544 | tf_op jit(solution)/shard_map/ppermute | solution.py:23
  179.2 22.3 %collective-permute-start.18 = (f32[1,128]{1,0:T(1,128)S(1)}, f32[1,128]{1,0:T(1,128)S(1)}, u32[]{:S(2)}, u32[]{:S(2)}) collective-permute-start(f32[1,128]{1,0:T(1,128)S(1)} %get-tuple-element.262), channel_id=1, source_target_pairs={{24,0},{32,8},{40,16},{48,24},{56,32},{64,40},{72,48},{80,56},{88,... | collective-permute-start | bytes 1544 | tf_op jit(solution)/shard_map/ppermute | solution.py:23
  182.8 20.4 %collective-permute-start.19 = (f32[1,128]{1,0:T(1,128)S(1)}, f32[1,128]{1,0:T(1,128)S(1)}, u32[]{:S(2)}, u32[]{:S(2)}) collective-permute-start(f32[1,128]{1,0:T(1,128)S(1)} %get-tuple-element.261), channel_id=1, source_target_pairs={{32,0},{40,8},{48,16},{56,24},{64,32},{72,40},{80,48},{88,56},{96,... | collective-permute-start | bytes 1544 | tf_op jit(solution)/shard_map/ppermute | solution.py:23
  187.3 15.9 %collective-permute-start.20 = (f32[1,128]{1,0:T(1,128)S(1)}, f32[1,128]{1,0:T(1,128)S(1)}, u32[]{:S(2)}, u32[]{:S(2)}) collective-permute-start(f32[1,128]{1,0:T(1,128)S(1)} %get-tuple-element.260), channel_id=1, source_target_pairs={{40,0},{48,8},{56,16},{64,24},{72,32},{80,40},{88,48},{96,56},{104... | collective-permute-start | bytes 1544 | tf_op jit(solution)/shard_map/ppermute | solution.py:23
  194.6 8.6 %collective-permute-start.21 = (f32[1,128]{1,0:T(1,128)S(1)}, f32[1,128]{1,0:T(1,128)S(1)}, u32[]{:S(2)}, u32[]{:S(2)}) collective-permute-start(f32[1,128]{1,0:T(1,128)S(1)} %get-tuple-element.259), channel_id=1, source_target_pairs={{48,0},{56,8},{64,16},{72,24},{80,32},{88,40},{96,48},{104,56},{11... | collective-permute-start | bytes 1544 | tf_op jit(solution)/shard_map/ppermute | solution.py:23
  199.6 7.6 %collective-permute-start.22 = (f32[1,128]{1,0:T(1,128)S(1)}, f32[1,128]{1,0:T(1,128)S(1)}, u32[]{:S(2)}, u32[]{:S(2)}) collective-permute-start(f32[1,128]{1,0:T(1,128)S(1)} %get-tuple-element.258), channel_id=1, source_target_pairs={{56,0},{64,8},{72,16},{80,24},{88,32},{96,40},{104,48},{112,56},{1... | collective-permute-start | bytes 1544 | tf_op jit(solution)/shard_map/ppermute | solution.py:23
  201.5 5.6 %collective-permute-start.23 = (f32[1,128]{1,0:T(1,128)S(1)}, f32[1,128]{1,0:T(1,128)S(1)}, u32[]{:S(2)}, u32[]{:S(2)}) collective-permute-start(f32[1,128]{1,0:T(1,128)S(1)} %get-tuple-element.264), channel_id=1, source_target_pairs={{64,0},{72,8},{80,16},{88,24},{96,32},{104,40},{112,48},{120,56},{... | collective-permute-start | bytes 1544 | tf_op jit(solution)/shard_map/ppermute | solution.py:23
Sparse Core Ops, SparseCore 0:
  67.2 94.1 all-reduce.1
